TPU v7x, 128 devices: a whole 4x4x4 slice. The times are simulated.
128 devices in a mesh: inp: 8 (over z_lo, y), chan: 16 (over z_hi, x, core).
Axes of the slice: x: 4, y: 4, z: 4 (z_hi: 2, z_lo: 2; z = z_hi * 2 + z_lo), core: 2. Of those that a mesh axis runs over, the one named last changes fastest.
Arguments:
- voltages: bfloat16 [256, 256, 8192], P('inp', 'chan'), may hold values from -6 to 6
- history: bfloat16 [256, 7, 8192], P('inp'), may hold values from -6 to 6
- taper: float32 [8, 8192], replicated, may hold values from -2 to 2
Outputs:
- visibility: bfloat16 [2, 2048, 256, 256], P(None, ('inp', 'chan'))
All inputs are finite; a program needn't handle non-finite values.
Results may differ from a plain program's by a relative error of at most 0.005.
Values may be sent and summed in bfloat16 or wider, within the bound.
A program may use at most 192 MiB of HBM per device.

v0:
```python
import math

import jax
import jax.numpy as jnp
from jax import lax
from jax.sharding import PartitionSpec as P

BAND = 2048
LOW = 1024


def shifted(value, axis, by):
    devices = lax.axis_size(axis)
    pairs = [(i, i + by) for i in range(devices) if 0 <= i + by < devices]
    return lax.ppermute(value, axis, pairs)


def tables(length, rows, cols):
    index = (
        jnp.arange(rows, dtype=jnp.int32)[:, None]
        * jnp.arange(cols, dtype=jnp.int32)[None, :]
        % length
    )
    angle = index.astype(jnp.float32) * (2.0 * math.pi / length)
    return (jnp.cos(angle), jnp.sin(angle))


def transform(filtered):
    in_dev, block_s, frame = filtered.shape
    radix = 128
    inner = frame // radix
    keep = inner // 2
    highest = lax.Precision.HIGHEST
    frames = filtered.reshape(in_dev, block_s, radix, inner)
    first_cos, first_sin = tables(radix, radix, radix)
    section_real = jnp.einsum("isan,ak->nksi", frames, first_cos, precision=highest)
    section_imag = -jnp.einsum("isan,ak->nksi", frames, first_sin, precision=highest)
    twist_cos, twist_sin = tables(frame, inner, radix)
    twist_cos = twist_cos[:, :, None, None]
    twist_sin = twist_sin[:, :, None, None]
    turned_real = section_real * twist_cos + section_imag * twist_sin
    turned_imag = section_imag * twist_cos - section_real * twist_sin
    second_cos, second_sin = tables(inner, inner, keep)
    final_real = jnp.einsum(
        "nksi,nm->mksi", turned_real, second_cos, precision=highest
    ) + jnp.einsum("nksi,nm->mksi", turned_imag, second_sin, precision=highest)
    final_imag = jnp.einsum(
        "nksi,nm->mksi", turned_imag, second_cos, precision=highest
    ) - jnp.einsum("nksi,nm->mksi", turned_real, second_sin, precision=highest)
    scale_factor = 1.0 / math.sqrt(frame)
    nch = keep * radix
    final_real = final_real.reshape(nch, block_s, in_dev)[LOW : LOW + BAND]
    final_imag = final_imag.reshape(nch, block_s, in_dev)[LOW : LOW + BAND]
    return (
        (final_real * scale_factor).astype(jnp.bfloat16),
        (final_imag * scale_factor).astype(jnp.bfloat16),
    )


def on_device(voltages, history, taper):
    in_dev, s_dev, frame = voltages.shape
    taps = taper.shape[0]
    n_inp = lax.axis_size("inp")
    n_chan = lax.axis_size("chan")
    tail = voltages[:, s_dev - (taps - 1) :, :]
    earlier = shifted(tail, "chan", 1)
    earlier = jnp.where(lax.axis_index("chan") == 0, history, earlier)
    extended = jnp.concatenate([earlier, voltages], axis=1)
    block_s = math.gcd(s_dev, max(1, 256 // in_dev))
    steps_count = s_dev // block_s
    band = BAND

    def filter_step(step_index, buffers):
        real_buf, imag_buf = buffers
        first = (step_index * block_s).astype(jnp.int32)
        slab = lax.dynamic_slice_in_dim(extended, first, block_s + taps - 1, axis=1)
        filtered = jnp.zeros((in_dev, block_s, frame), jnp.float32)
        for offset in range(taps):
            filtered = (
                filtered + taper[offset][None, None, :] * slab[:, offset : offset + block_s, :]
            )
        real_out, imag_out = transform(filtered)
        real_buf = lax.dynamic_update_slice_in_dim(real_buf, real_out, first, axis=1)
        imag_buf = lax.dynamic_update_slice_in_dim(imag_buf, imag_out, first, axis=1)
        return (real_buf, imag_buf)

    empty = jnp.zeros((band, s_dev, in_dev), jnp.bfloat16)
    real_all, imag_all = lax.fori_loop(0, steps_count, filter_step, (empty, empty))
    groups = n_inp * n_chan
    ch_dev = band // groups
    total_inputs = n_inp * in_dev
    spectra_count = n_chan * s_dev
    real_send = real_all.reshape(groups, 1, ch_dev, s_dev, in_dev)
    imag_send = imag_all.reshape(groups, 1, ch_dev, s_dev, in_dev)
    real_got, imag_got = (
        lax.all_to_all(real_send, ("inp", "chan"), split_axis=0, concat_axis=1, tiled=True),
        lax.all_to_all(imag_send, ("inp", "chan"), split_axis=0, concat_axis=1, tiled=True),
    )
    real_part = real_got.reshape(n_inp, n_chan, ch_dev, s_dev, in_dev)
    imag_part = imag_got.reshape(n_inp, n_chan, ch_dev, s_dev, in_dev)

    def correlate(left, right):
        return jnp.einsum(
            "acksi,bcksj->kaibj", left, right, preferred_element_type=jnp.float32
        ).reshape(ch_dev, total_inputs, total_inputs)

    vis_real = correlate(real_part, real_part) + correlate(imag_part, imag_part)
    vis_imag = correlate(imag_part, real_part) - correlate(real_part, imag_part)
    stacked = jnp.stack([vis_real, vis_imag])
    return (stacked / spectra_count).astype(jnp.bfloat16)


def solution(mesh):
    in_specs = (P("inp", "chan", None), P("inp", None, None), P())
    out_specs = P(None, ("inp", "chan"), None, None)
    return jax.shard_map(
        on_device, mesh=mesh, in_specs=in_specs, out_specs=out_specs, check_vma=False
    )
```

profile of v0, /device:TPU:1, one launch (start us, length us, event | category | flops | bytes accessed | tf_op | source)
XLA Modules:
  0.0 600.0 jit_solution(14866745671155337925)
XLA Ops:
  0.0 3.1 slice.203
  3.1 4.1 copy.56
  7.3 4.5 collective-permute-start
  11.8 40.1 %collective-permute-done = bf16[32,7,8192]{2,0,1:T(8,128)(2,1)} collective-permute-done((bf16[32,7,8192]{2,0,1:T(8,128)(2,1)}, bf16[32,7,8192]{2,0,1:T(8,128)(2,1)}, u32[]{:S(2)}, u32[]{:S(2)}) %collective-permute-start) | collective-permute-done | bytes 3670048 | tf_op jit(solution)/shard_map/ppermute | solution.py:15
  51.9 2.4 broadcast_select_fusion
  54.3 2.0 copy.33
  56.4 10.5 %pad_maximum_fusion = bf16[32,23,8192]{2,1,0:T(8,128)(2,1)} fusion(bf16[32,16,8192]{2,1,0:T(8,128)(2,1)} %param.5, bf16[32,7,8192]{2,1,0:T(8,128)(2,1)S(1)} %copy.33), kind=kLoop, calls=%fused_computation.90 | loop fusion | flops 24117248 | bytes 24117248 | tf_op jit(solution)/shard_map/concatenate | solution.py:68
  66.9 1.6 broadcast_in_dim.23.clone
  68.5 1.6 broadcast_in_dim.23
  70.1 273.1 %while.18 = (s32[]{:T(128)}, bf16[2048,16,32]{0,2,1:T(8,128)(2,1)}, bf16[2048,16,32]{0,2,1:T(8,128)(2,1)}, f32[8,8192]{1,0:T(8,128)S(1)}, bf16[32,23,8192]{2,1,0...) while((s32[]{:T(128)}, bf16[2048,16,32]{0,2,1:T(8,128)(2,1)}, ...), condition=%wide.region_1.2_spmd, body=%wide.region_0.1_spmd.sunk | while | flops 9730539520 | bytes 237896112 | solution.py:88
  70.8 27.8 %multiply_add_fusion.2 = f32[32,8,8192]{2,1,0:T(8,128)} fusion(bf16[32,23,8192]{2,1,0:T(8,128)(2,1)} %get-tuple-element.281, s32[]{:T(128)S(6)} %add.336, s32[]{:T(128)S(6)} %add.337, s32[]{:T(128)S(6)} %add.338, s32[]{:T(128)S(6)} %add.339, s32[]{:T(128)S(6)} %add.340, s32[]{:T(128)S(6)} %add.341, s32[]{:T(128)S(6)} %add.342, s32[]{:T(128)S(6)} %select_n.183, ...), kind=kLoop, calls=%fused_computation.6.clone.1 | loop fusion | flops 48234496 | bytes 42205216 | tf_op jit(solution)/shard_map/while/body/eval_jaxpr/add | solution.py:80
  98.6 14.2 %reshape.155 = f32[32,8,128,64]{3,2,1,0:T(8,128)} reshape(f32[32,8,8192]{2,1,0:T(8,128)} %multiply_add_fusion.2) | data formatting | bytes 16777216 | tf_op jit(solution)/shard_map/while/body/eval_jaxpr/reshape | solution.py:34
  112.8 32.2 %fusion.124 = f32[128,32,8,64]{0,3,2,1:T(8,128)} fusion(f32[32,8,128,64]{3,2,1,0:T(8,128)} %reshape.155), kind=kOutput, calls=%fused_computation.27.clone.1 | convolution fusion | flops 3221454848 | bytes 16777216 | tf_op jit(solution)/shard_map/while/body/eval_jaxpr/isan,ak->nksi/dot_general | solution.py:37
  144.9 34.7 %fusion.127 = (f32[64,128,8,32]{1,0,2,3:T(8,128)}, f32[64,128,8,32]{1,0,2,3:T(8,128)}) fusion(f32[128,32,8,64]{0,3,2,1:T(8,128)} %fusion.124, f32[64,128]{1,0:T(8,128)S(1)} %fusion.125, f32[64,128]{1,0:T(8,128)S(1)} %fusion.126, f32[32,8,128,64]{3,2,1,0:T(8,128)} %reshape.155), kind=kOutput, calls=%fused_computation.2.clone.1 | convolution fusion | flops 3236134912 | bytes 33619968 | tf_op jit(solution)/shard_map/while/body/eval_jaxpr/isan,ak->nksi/dot_general | solution.py:36
  179.7 6.7 %fusion.132 = f32[32,128,8,32]{1,0,3,2:T(8,128)S(1)} fusion(f32[64,128,8,32]{1,0,2,3:T(8,128)} %get-tuple-element.239), kind=kOutput, calls=%fused_computation.13.clone.1 | convolution fusion | flops 805335040 | bytes 12582912 | tf_op jit(solution)/shard_map/while/body/eval_jaxpr/nksi,nm->mksi/dot_general | solution.py:44
  186.4 4.5 fusion.128
  191.0 4.5 fusion.131
  196.0 4.9 fusion.129
  202.4 1.5 constant_dynamic-update-slice_fusion.3
  204.5 28.2 %multiply_add_fusion.2 = f32[32,8,8192]{2,1,0:T(8,128)} fusion(bf16[32,23,8192]{2,1,0:T(8,128)(2,1)} %get-tuple-element.281, s32[]{:T(128)S(6)} %add.336, s32[]{:T(128)S(6)} %add.337, s32[]{:T(128)S(6)} %add.338, s32[]{:T(128)S(6)} %add.339, s32[]{:T(128)S(6)} %add.340, s32[]{:T(128)S(6)} %add.341, s32[]{:T(128)S(6)} %add.342, s32[]{:T(128)S(6)} %select_n.183, ...), kind=kLoop, calls=%fused_computation.6.clone.1 | loop fusion | flops 48234496 | bytes 42205216 | tf_op jit(solution)/shard_map/while/body/eval_jaxpr/add | solution.py:80
  232.7 14.2 %reshape.155 = f32[32,8,128,64]{3,2,1,0:T(8,128)} reshape(f32[32,8,8192]{2,1,0:T(8,128)} %multiply_add_fusion.2) | data formatting | bytes 16777216 | tf_op jit(solution)/shard_map/while/body/eval_jaxpr/reshape | solution.py:34
  246.9 31.9 %fusion.124 = f32[128,32,8,64]{0,3,2,1:T(8,128)} fusion(f32[32,8,128,64]{3,2,1,0:T(8,128)} %reshape.155), kind=kOutput, calls=%fused_computation.27.clone.1 | convolution fusion | flops 3221454848 | bytes 16777216 | tf_op jit(solution)/shard_map/while/body/eval_jaxpr/isan,ak->nksi/dot_general | solution.py:37
  278.8 34.9 %fusion.127 = (f32[64,128,8,32]{1,0,2,3:T(8,128)}, f32[64,128,8,32]{1,0,2,3:T(8,128)}) fusion(f32[128,32,8,64]{0,3,2,1:T(8,128)} %fusion.124, f32[64,128]{1,0:T(8,128)S(1)} %fusion.125, f32[64,128]{1,0:T(8,128)S(1)} %fusion.126, f32[32,8,128,64]{3,2,1,0:T(8,128)} %reshape.155), kind=kOutput, calls=%fused_computation.2.clone.1 | convolution fusion | flops 3236134912 | bytes 33619968 | tf_op jit(solution)/shard_map/while/body/eval_jaxpr/isan,ak->nksi/dot_general | solution.py:36
  313.7 6.7 %fusion.132 = f32[32,128,8,32]{1,0,3,2:T(8,128)S(1)} fusion(f32[64,128,8,32]{1,0,2,3:T(8,128)} %get-tuple-element.239), kind=kOutput, calls=%fused_computation.13.clone.1 | convolution fusion | flops 805335040 | bytes 12582912 | tf_op jit(solution)/shard_map/while/body/eval_jaxpr/nksi,nm->mksi/dot_general | solution.py:44
  320.5 4.5 fusion.128
  325.0 4.5 fusion.131
  330.0 4.7 fusion.129
  343.2 10.0 %copy.37 = bf16[2048,16,32]{2,1,0:T(8,128)(2,1)} copy(bf16[2048,16,32]{0,2,1:T(8,128)(2,1)} %get-tuple-element.165) | data formatting | bytes 4194304 | tf_op jit(solution)/shard_map/while | solution.py:88
  353.2 12.8 %reshape.150 = bf16[128,2,4096]{2,1,0:T(2,128)(2,1)} reshape(bf16[128,1,16,16,32]{4,3,2,1,0:T(8,128)(2,1)} %bitcast.148) | data formatting | bytes 4194304
  366.0 12.5 %all-to-all-start.1 = ((bf16[128,2,4096]{2,1,0:T(2,128)(2,1)}), bf16[128,2,4096]{2,1,0:T(2,128)(2,1)S(1)}, u32[]{:S(2)}, u32[]{:S(2)}) async-start(bf16[128,2,4096]{2,1,0:T(2,128)(2,1)} %reshape.150), calls=%async_computation.1 | async-start | bytes 4194304 | tf_op jit(solution)/shard_map/all_to_all | solution.py:97
  378.5 10.0 %copy.34 = bf16[2048,16,32]{2,1,0:T(8,128)(2,1)} copy(bf16[2048,16,32]{0,2,1:T(8,128)(2,1)} %get-tuple-element.164) | data formatting | bytes 4194304 | tf_op jit(solution)/shard_map/while | solution.py:88
  388.5 12.8 %reshape.152 = bf16[128,2,4096]{2,1,0:T(2,128)(2,1)} reshape(bf16[128,1,16,16,32]{4,3,2,1,0:T(8,128)(2,1)} %bitcast.149) | data formatting | bytes 4194304
  401.3 7.5 %all-to-all-done.1 = bf16[128,2,4096]{2,1,0:T(2,128)(2,1)S(1)} async-done(((bf16[128,2,4096]{2,1,0:T(2,128)(2,1)}), bf16[128,2,4096]{2,1,0:T(2,128)(2,1)S(1)}, u32[]{:S(2)}, u32[]{:S(2)}) %all-to-all-start.1) | async-done | bytes 2097184 | tf_op jit(solution)/shard_map/all_to_all | solution.py:97
  408.8 6.1 %all-to-all-start = ((bf16[128,2,4096]{2,1,0:T(2,128)(2,1)}), bf16[128,2,4096]{2,1,0:T(2,128)(2,1)}, u32[]{:S(2)}, u32[]{:S(2)}) async-start(bf16[128,2,4096]{2,1,0:T(2,128)(2,1)} %reshape.152), calls=%async_computation | async-start | bytes 4194304 | tf_op jit(solution)/shard_map/all_to_all | solution.py:96
  414.9 6.5 %reshape.151 = bf16[128,1,16,16,32]{4,3,2,1,0:T(8,128)(2,1)} reshape(bf16[128,2,4096]{2,1,0:T(2,128)(2,1)S(1)} %all-to-all-done.1) | data formatting | bytes 4194304
  421.5 8.8 %copy.39 = bf16[128,1,16,16,32]{4,3,0,2,1:T(8,128)(2,1)} copy(bf16[128,1,16,16,32]{4,3,2,1,0:T(8,128)(2,1)} %reshape.151) | data formatting | bytes 4194304 | tf_op jit(solution)/shard_map/all_to_all | solution.py:97
  430.2 14.6 %all-to-all-done = bf16[128,2,4096]{2,1,0:T(2,128)(2,1)} async-done(((bf16[128,2,4096]{2,1,0:T(2,128)(2,1)}), bf16[128,2,4096]{2,1,0:T(2,128)(2,1)}, u32[]{:S(2)}, u32[]{:S(2)}) %all-to-all-start) | async-done | bytes 2097184 | tf_op jit(solution)/shard_map/all_to_all | solution.py:96
  444.8 11.4 %reshape.153 = bf16[128,1,16,16,32]{4,3,2,1,0:T(8,128)(2,1)} reshape(bf16[128,2,4096]{2,1,0:T(2,128)(2,1)} %all-to-all-done) | data formatting | bytes 4194304
  456.2 8.8 %copy.36 = bf16[128,1,16,16,32]{4,3,0,2,1:T(8,128)(2,1)} copy(bf16[128,1,16,16,32]{4,3,2,1,0:T(8,128)(2,1)} %reshape.153) | data formatting | bytes 4194304 | tf_op jit(solution)/shard_map/all_to_all | solution.py:96
  465.0 13.9 %fusion.78 = f32[16,8,32,8,32,1]{4,2,5,3,1,0:T(8,128)} fusion(bf16[8,16,16,16,32,1]{4,3,1,5,0,2:T(8,128)(2,1)} %bitcast.145, bf16[8,16,16,16,32,1]{4,3,1,0,5,2:T(8,128)(2,1)} %bitcast.144), kind=kOutput, calls=%fused_computation.95 | convolution fusion | flops 536870912 | bytes 8388608 | tf_op jit(solution)/shard_map/acksi,bcksj->kaibj/dot_general | solution.py:103
  479.0 14.0 %fusion.79 = f32[16,8,32,8,32,1]{4,2,5,3,1,0:T(8,128)} fusion(bf16[8,16,16,16,32,1]{4,3,1,5,0,2:T(8,128)(2,1)} %bitcast.140, bf16[8,16,16,16,32,1]{4,3,1,0,5,2:T(8,128)(2,1)} %bitcast.146), kind=kOutput, calls=%fused_computation.96 | convolution fusion | flops 536870912 | bytes 8388608 | tf_op jit(solution)/shard_map/acksi,bcksj->kaibj/dot_general | solution.py:103
  492.9 17.5 %bitcast_add_fusion = f32[16,8,32,8,32]{4,2,3,1,0:T(8,128)} fusion(f32[16,8,32,8,32,1]{4,2,5,3,1,0:T(8,128)} %fusion.78, bf16[8,16,16,16,32,1]{4,3,1,5,0,2:T(8,128)(2,1)} %bitcast.141, bf16[8,16,16,16,32,1]{4,3,1,0,5,2:T(8,128)(2,1)} %bitcast.142), kind=kOutput, calls=%fused_computation.89 | convolution fusion | flops 537919488 | bytes 12582912 | tf_op jit(solution)/shard_map/acksi,bcksj->kaibj/dot_general | solution.py:103
  510.4 21.2 %copy.40 = f32[16,8,32,8,32]{4,3,2,1,0:T(8,128)} copy(f32[16,8,32,8,32]{4,2,3,1,0:T(8,128)} %bitcast_add_fusion) | data formatting | bytes 8388608 | tf_op jit(solution)/shard_map/add | solution.py:107
  531.6 12.2 %add.225 = f32[1,16,256,256]{3,2,1,0:T(8,128)} reshape(f32[16,8,32,8,32]{4,3,2,1,0:T(8,128)} %copy.40) | data formatting | bytes 8388608 | tf_op jit(solution)/shard_map/add | solution.py:107
  543.8 17.5 %bitcast_subtract_fusion = f32[16,8,32,8,32]{4,2,3,1,0:T(8,128)} fusion(f32[16,8,32,8,32,1]{4,2,5,3,1,0:T(8,128)} %fusion.79, bf16[8,16,16,16,32,1]{4,3,1,5,0,2:T(8,128)(2,1)} %bitcast.147, bf16[8,16,16,16,32,1]{4,3,1,0,5,2:T(8,128)(2,1)} %bitcast.143), kind=kOutput, calls=%fused_computation.88 | convolution fusion | flops 537919488 | bytes 12582912 | tf_op jit(solution)/shard_map/acksi,bcksj->kaibj/dot_general | solution.py:103
  561.3 21.0 %copy.41 = f32[16,8,32,8,32]{4,3,2,1,0:T(8,128)} copy(f32[16,8,32,8,32]{4,2,3,1,0:T(8,128)} %bitcast_subtract_fusion) | data formatting | bytes 8388608 | tf_op jit(solution)/shard_map/sub | solution.py:108
  582.3 12.2 %sub.36 = f32[1,16,256,256]{3,2,1,0:T(8,128)} reshape(f32[16,8,32,8,32]{4,3,2,1,0:T(8,128)} %copy.41) | data formatting | bytes 8388608 | tf_op jit(solution)/shard_map/sub | solution.py:108
  594.5 5.3 fusion.76
  (31 shorter events, 6.5 us)
Async XLA Ops:
  7.3 44.6 %collective-permute-start = (bf16[32,7,8192]{2,0,1:T(8,128)(2,1)}, bf16[32,7,8192]{2,0,1:T(8,128)(2,1)}, u32[]{:S(2)}, u32[]{:S(2)}) collective-permute-start(bf16[32,7,8192]{2,0,1:T(8,128)(2,1)} %copy.56), channel_id=1, source_target_pairs={{0,1},{1,2},{2,3},{3,4},{4,5},{5,6},{6,7},{7,8},{8,9},{9,10},{10,1... | collective-permute-start | bytes 11010056 | tf_op jit(solution)/shard_map/ppermute | solution.py:15
  56.4 13.7 %copy-start.1 = (f32[8,8192]{1,0:T(8,128)S(1)}, f32[8,8192]{1,0:T(8,128)}, u32[]{:S(2)}) copy-start(f32[8,8192]{1,0:T(8,128)} %param.7) | copy-start | bytes 786436
  179.7 6.7 %copy-start = (f32[64,128,8,32]{1,0,2,3:T(8,128)S(1)}, f32[64,128,8,32]{1,0,2,3:T(8,128)}, u32[]{:S(2)}) copy-start(f32[64,128,8,32]{1,0,2,3:T(8,128)} %get-tuple-element.239) | copy-start | bytes 25165828 | tf_op jit(solution)/shard_map/while
  179.7 11.2 %slice-start = ((s8[8388608]{0:T(1024)(128)(4,1)}), s8[4194304]{0:T(1024)(128)(4,1)S(1)}, s32[]{:S(2)}) async-start(s8[8388608]{0:T(1024)(128)(4,1)} %bitcast.138), calls=%async_computation.2 | async-start | bytes 8388608 | tf_op jit(solution)/shard_map/while
  186.4 4.5 slice-start.1
  313.7 6.7 %copy-start = (f32[64,128,8,32]{1,0,2,3:T(8,128)S(1)}, f32[64,128,8,32]{1,0,2,3:T(8,128)}, u32[]{:S(2)}) copy-start(f32[64,128,8,32]{1,0,2,3:T(8,128)} %get-tuple-element.239) | copy-start | bytes 25165828 | tf_op jit(solution)/shard_map/while
  313.7 11.2 %slice-start = ((s8[8388608]{0:T(1024)(128)(4,1)}), s8[4194304]{0:T(1024)(128)(4,1)S(1)}, s32[]{:S(2)}) async-start(s8[8388608]{0:T(1024)(128)(4,1)} %bitcast.138), calls=%async_computation.2 | async-start | bytes 8388608 | tf_op jit(solution)/shard_map/while
  320.4 4.5 slice-start.1
  366.0 42.8 %all-to-all-start.1 = ((bf16[128,2,4096]{2,1,0:T(2,128)(2,1)}), bf16[128,2,4096]{2,1,0:T(2,128)(2,1)S(1)}, u32[]{:S(2)}, u32[]{:S(2)}) async-start(bf16[128,2,4096]{2,1,0:T(2,128)(2,1)} %reshape.150), calls=%async_computation.1 | async-start | bytes 4194304 | tf_op jit(solution)/shard_map/all_to_all | solution.py:97
  408.8 36.0 %all-to-all-start = ((bf16[128,2,4096]{2,1,0:T(2,128)(2,1)}), bf16[128,2,4096]{2,1,0:T(2,128)(2,1)}, u32[]{:S(2)}, u32[]{:S(2)}) async-start(bf16[128,2,4096]{2,1,0:T(2,128)(2,1)} %reshape.152), calls=%async_computation | async-start | bytes 4194304 | tf_op jit(solution)/shard_map/all_to_all | solution.py:96
where the time goes:
time: 608 us; the launch traced here: 600 us
  matrix products  238 us (39%)
  local copies, waits for them, and re-layouts  194 us (32%)
  other arithmetic  76.9 us (13%)
  waiting for transfers between devices  62.2 us (10%)
  starting transfers between devices  23.1 us (4%)
  loops' own time  6.22 us (1%)
    dot_general x2, matrix products, transform(): jnp.einsum('isan,ak->nksi', frames, first_cos, precision=highest)  69.7 us
    dot_general x2, matrix products, transform(): jnp.einsum('isan,ak->nksi', frames, first_sin, precision=highest)  64 us
    dot_general x4, matrix products, correlate(): jnp.einsum('acksi,bcksj->kaibj', left, right, preferred_element_type=jnp....  63 us
    add x2, other arithmetic, filter_step(): filtered + taper[offset][None, None, :] * slab[:, offset:offset + block_s...  56 us
    unnamed x7, local copies, waits for them, and re-layouts  47.7 us
    ppermute x1, waiting for transfers between devices, shifted(): return lax.ppermute(value, axis, pairs)  40.1 us
    add x2, local copies, waits for them, and re-layouts, on_device(): vis_real = correlate(real_part, real_part) + correlate(imag_part, imag_part)  33.3 us
    sub x2, local copies, waits for them, and re-layouts, on_device(): vis_imag = correlate(imag_part, real_part) - correlate(real_part, imag_part)  33.1 us
  transfers between devices with their start and end apart: 3, of which 3 were waited for; matrix products, arithmetic and copies ran while one was open for 6% of the time, Pallas kernels for 0%

commit v1 on v0

v1 whole, which is shorter than its diff:
```python
import functools
import math

import jax
import jax.numpy as jnp
import ml_dtypes
import numpy as np
from jax import lax
from jax.experimental import pallas as pl
from jax.experimental.pallas import tpu as pltpu
from jax.sharding import PartitionSpec as P

FRAME = 8192
LOW = 1024
BAND = 2048
TAPS = 8
RADIX = 32
INNER = FRAME // RADIX
LANES = 128
NIN = 32
SPECTRA = 16
STRIDE = 16
COLS = FRAME // LANES
SLOTS = 4


def second_stage_tables():
    m = np.arange(INNER, dtype=np.int64)
    k1 = LOW // RADIX + np.arange(BAND // RADIX, dtype=np.int64)

    def angles(k0):
        index = (m[None, :] * (k0 + RADIX * k1[:, None])) % FRAME
        angle = index * (2.0 * math.pi / FRAME)
        return np.cos(angle), np.sin(angle)

    table = np.zeros((RADIX // 2, 4, k1.size, 2, INNER))
    for k0 in range(1, RADIX // 2):
        cos, sin = angles(k0)
        table[k0, 0, :, 0], table[k0, 0, :, 1] = cos, sin
        table[k0, 1, :, 0], table[k0, 1, :, 1] = -sin, cos
        cos, sin = angles(RADIX - k0)
        table[k0, 2, :, 0], table[k0, 2, :, 1] = cos, -sin
        table[k0, 3, :, 0], table[k0, 3, :, 1] = -sin, -cos
    cos, sin = angles(0)
    table[0, 0, :, 0], table[0, 1, :, 0] = cos, -sin
    cos, sin = angles(RADIX // 2)
    table[0, 2, :, 1], table[0, 3, :, 1] = cos, -sin
    table = (table / math.sqrt(FRAME)).reshape(RADIX // 2, 4 * k1.size, 2 * INNER)
    table = table.astype(np.float32)
    high = table.astype(ml_dtypes.bfloat16)
    low = (table - high.astype(np.float32)).astype(ml_dtypes.bfloat16)
    return high, low


def real_fft(values):
    n = len(values)
    if n == 2:
        return [values[0] + values[1], values[0] - values[1]], [None, None]
    even_re, even_im = real_fft(values[0::2])
    odd_re, odd_im = real_fft(values[1::2])
    re, im = [None] * (n // 2 + 1), [None] * (n // 2 + 1)
    re[0], re[n // 2] = even_re[0] + odd_re[0], even_re[0] - odd_re[0]
    re[n // 4], im[n // 4] = even_re[n // 4], -odd_re[n // 4]
    for k in range(1, n // 4):
        cos, sin = math.cos(2 * math.pi * k / n), math.sin(2 * math.pi * k / n)
        if 8 * k == n:
            turned_re = (odd_re[k] + odd_im[k]) * cos
            turned_im = (odd_im[k] - odd_re[k]) * cos
        else:
            turned_re = odd_re[k] * cos + odd_im[k] * sin
            turned_im = odd_im[k] * cos - odd_re[k] * sin
        re[k], im[k] = even_re[k] + turned_re, even_im[k] + turned_im
        re[n // 2 - k], im[n // 2 - k] = even_re[k] - turned_re, turned_im - even_im[k]
    return re, im


def spectra_kernel(
    edges, own_hbm, taper, high_hbm, low_hbm, *rest
):
    if edges:
        left_hbm, right_hbm, history_hbm, out, own, left, right, history, *rest = rest
    else:
        out, own, *rest = rest
    high, low, rows, filtered, turned, gathered, sems = rest
    copies = [pltpu.make_async_copy(own_hbm.at[pl.ds(16 * g, 16)], own.at[pl.ds(16 * g, 16)], sems.at[g]) for g in range(2)]
    if edges:
        copies.append(pltpu.make_async_copy(left_hbm, left, sems.at[2]))
        copies.append(pltpu.make_async_copy(right_hbm, right, sems.at[3]))
        copies.append(pltpu.make_async_copy(history_hbm, history, sems.at[4]))
    tables = [pltpu.make_async_copy(high_hbm, high, sems.at[5]), pltpu.make_async_copy(low_hbm, low, sems.at[6])]
    for copy in copies + tables:
        copy.start()
    for copy in copies:
        copy.wait()
    if edges:
        first = lax.axis_index("chan") == 0
        last = lax.axis_index("chan") == lax.axis_size("chan") - 1

    def column(group, col, slot):
        base = slot * 16 * STRIDE
        lanes = pl.ds(pl.multiple_of(col * LANES, LANES), LANES)
        for i in range(16):
            rows[pl.ds(base + i * STRIDE, 16), :] = own[group * 16 + i, :, lanes].astype(jnp.float32)

    def fir(group, col, slot):
        base = slot * 16 * STRIDE
        lanes = pl.ds(pl.multiple_of(col * LANES, LANES), LANES)
        taps = taper[:, lanes]
        taps = [jnp.broadcast_to(taps[t : t + 1], (8, LANES)) for t in range(TAPS)]
        if edges:
            inputs = pl.ds(pl.multiple_of(group * 16, 16), 16)
            past = [history[f, inputs, lanes].astype(jnp.float32) for f in range(7)]
            before = [left[f, inputs, lanes].astype(jnp.float32) for f in range(4)]
            before = [jnp.where(first, past[3 + f], before[f]) for f in range(4)]
            after = [right[f, inputs, lanes].astype(jnp.float32) for f in range(3)]
        for h in range(2):
            def frame(f):
                return rows[pl.ds(base + 8 * h * STRIDE + f, 8, stride=STRIDE), :]

            def half(value):
                return value[8 * h : 8 * h + 8]

            if edges:
                near = [frame(f) for f in range(16) if f != 7]
                start = [half(b) for b in before] + near[:7]
                tail = near[7:]
                end = [jnp.where(last, half(past[f]), tail[1 + f]) for f in range(7)] + [half(a) for a in after]
                windows = [start[o : o + TAPS] for o in range(4)] + [tail] + [end[o : o + TAPS] for o in range(3)]
            else:
                near = [frame(f) for f in range(15)]
                windows = [near[o : o + TAPS] for o in range(8)]
            for o, window in enumerate(windows):
                total = window[0] * taps[0]
                for t in range(1, TAPS):
                    total = total + window[t] * taps[t]
                filtered[o, col, pl.ds(8 * h, 8), :] = total

    def group_step(group, carry):
        def columns(step, carry):
            for slot in range(SLOTS):
                column(group, step * SLOTS + slot, slot)
            for slot in range(SLOTS):
                fir(group, step * SLOTS + slot, slot)
            return carry

        lax.fori_loop(0, COLS // SLOTS, columns, 0)

        def first_stage(o, carry):
            for part in range(2):
                for h in range(2):
                    values = [filtered[o, 2 * a + part, pl.ds(8 * h, 8), :] for a in range(RADIX)]
                    re, im = real_fft(values)
                    im[0] = re[RADIX // 2]
                    row = pl.ds(pl.multiple_of(o * NIN + group * 16 + 8 * h, 8), 8)
                    for k in range(RADIX // 2):
                        turned[2 * k, row, part * LANES : (part + 1) * LANES] = re[k]
                        turned[2 * k + 1, row, part * LANES : (part + 1) * LANES] = im[k]
            return carry

        lax.fori_loop(0, 8, first_stage, 0)
        return carry

    lax.fori_loop(0, 2, group_step, 0)
    for copy in tables:
        copy.wait()

    def second_stage(k, carry):
        both = jnp.concatenate([turned[2 * k], turned[2 * k + 1]], axis=1)
        both_high = both.astype(jnp.bfloat16)
        both_low = (both - both_high.astype(jnp.float32)).astype(jnp.bfloat16)

        def product(table, value):
            return lax.dot_general(table, value, (((1,), (1,)), ((), ())), preferred_element_type=jnp.float32)

        result = product(high[k], both_high) + product(high[k], both_low) + product(low[k], both_high)
        other = lax.rem(RADIX // 2 - k, RADIX // 2)
        for block in range(4):
            begin = 32 * (block // 2) + 16 * (block % 2) + (other if block >= 2 else k)
            for tile in range(2):
                gathered[tile, pl.ds(begin, 64, stride=64), :] = result[
                    64 * block : 64 * block + 64, tile * LANES : (tile + 1) * LANES
                ]
        return carry

    lax.fori_loop(0, RADIX // 2, second_stage, 0)

    def emit(block, carry):
        for tile in range(2):
            value = gathered[tile, pl.ds(pl.multiple_of(block * 256, 256), 256), :].astype(jnp.bfloat16)
            out[pl.ds(block * 8, 8), tile] = value.reshape(8, 32, LANES)
        return carry

    lax.fori_loop(0, 16, emit, 0)


def spectra_half(edges, voltages, taper, high, low, *halo):
    any_space = pl.BlockSpec(memory_space=pl.ANY)
    vmem = pl.BlockSpec(memory_space=pltpu.VMEM)
    scratch = [pltpu.VMEM((NIN, SPECTRA, FRAME), jnp.bfloat16)]
    if edges:
        scratch += [pltpu.VMEM((f, NIN, FRAME), jnp.bfloat16) for f in (4, 3, 7)]
    scratch += [
        pltpu.VMEM((16, 256, 512), jnp.bfloat16),
        pltpu.VMEM((16, 256, 512), jnp.bfloat16),
        pltpu.VMEM((SLOTS * 16 * STRIDE, LANES), jnp.float32),
        pltpu.VMEM((8, COLS, 16, LANES), jnp.float32),
        pltpu.VMEM((RADIX, 256, 256), jnp.float32),
        pltpu.VMEM((2, 4096, LANES), jnp.float32),
        pltpu.SemaphoreType.DMA((7,)),
    ]
    return pl.pallas_call(
        functools.partial(spectra_kernel, edges),
        out_shape=jax.ShapeDtypeStruct((128, 2, 32, LANES), jnp.bfloat16),
        in_specs=[any_space, vmem, any_space, any_space] + [any_space] * len(halo),
        out_specs=vmem,
        scratch_shapes=scratch,
        compiler_params=pltpu.CompilerParams(vmem_limit_bytes=58 << 20),
        cost_estimate=pl.CostEstimate(flops=20_000_000_000, bytes_accessed=20_000_000, transcendentals=0),
        name="spectra_edges" if edges else "spectra_inner",
    )(voltages, taper, high, low, *halo)


def correlate_kernel(first_ref, second_ref, out, rows, matrix):
    @pl.when(pl.program_id(0) == 0)
    def _():
        lane = lax.broadcasted_iota(jnp.int32, (16, LANES), 1)
        lower = lane < 64
        even = lane % 64 < 32
        for which, ref in enumerate((first_ref, second_ref)):
            def regroup(step, carry):
                tile, part, quad = step // 4, (step // 2) % 2, step % 2
                for a in range(4):
                    for src in range(16):
                        value = ref[(quad * 4 + a) * 16 + src, tile, pl.ds(pl.multiple_of(part * 16, 16), 16), :]
                        rows[pl.ds((a * 16 + src) * 16, 16), :] = value.astype(jnp.float32)
                for c in range(16):
                    t = [rows[pl.ds(a * 256 + c, 16, stride=16), :] for a in range(4)]
                    u = [None] * 4
                    for a in range(2):
                        u[a] = jnp.where(lower, t[a], pltpu.roll(t[a + 2], 64, 1))
                        u[a + 2] = jnp.where(lower, pltpu.roll(t[a], 64, 1), t[a + 2])
                    for a in (0, 2):
                        for b, value in enumerate(
                            (
                                jnp.where(even, u[a], pltpu.roll(u[a + 1], 32, 1)),
                                jnp.where(even, pltpu.roll(u[a], 96, 1), u[a + 1]),
                            )
                        ):
                            row = pl.ds(pl.multiple_of(((which * 2 + tile) * 4 + a + b) * 16, 16), 16)
                            lanes = pl.ds(pl.multiple_of(quad * LANES, LANES), LANES)
                            matrix[c, part, row, lanes] = value.astype(jnp.bfloat16)
                return carry

            lax.fori_loop(0, 8, regroup, 0)

    c = pl.program_id(0)
    re, im = matrix[c, 0], matrix[c, 1]

    def product(left, right):
        return lax.dot_general(left, right, (((0,), (0,)), ((), ())), preferred_element_type=jnp.float32)

    scale = 1.0 / 256.0
    out[0, 0] = ((product(re, re) + product(im, im)) * scale).astype(jnp.bfloat16)
    out[1, 0] = ((product(im, re) - product(re, im)) * scale).astype(jnp.bfloat16)


def correlate(first, second):
    shape = first.shape
    whole = pl.BlockSpec(shape, lambda c: (0, 0, 0, 0), pipeline_mode=pl.Buffered(1))
    return pl.pallas_call(
        correlate_kernel,
        grid=(16,),
        out_shape=jax.ShapeDtypeStruct((2, 16, 256, 256), jnp.bfloat16),
        in_specs=[whole, whole],
        out_specs=pl.BlockSpec((2, 1, 256, 256), lambda c: (0, c, 0, 0)),
        scratch_shapes=[pltpu.VMEM((1024, LANES), jnp.float32), pltpu.VMEM((16, 2, 256, 256), jnp.bfloat16)],
        compiler_params=pltpu.CompilerParams(vmem_limit_bytes=40 << 20),
        cost_estimate=pl.CostEstimate(flops=4_300_000_000, bytes_accessed=9_000_000, transcendentals=0),
        name="correlate",
    )(first, second)


def on_device(voltages, history, taper):
    high, low = (jnp.asarray(t) for t in second_stage_tables())
    chan = lax.axis_size("chan")
    left = jnp.transpose(voltages[:, SPECTRA - 4 :], (1, 0, 2))
    right = jnp.transpose(voltages[:, :3], (1, 0, 2))
    left = lax.ppermute(left, "chan", [(i, i + 1) for i in range(chan - 1)])
    right = lax.ppermute(right, "chan", [(i, (i - 1) % chan) for i in range(chan)])
    history = jnp.transpose(history, (1, 0, 2))

    def exchange(value):
        return lax.all_to_all(value, ("inp", "chan"), split_axis=0, concat_axis=0, tiled=True)

    inner = exchange(spectra_half(False, voltages, taper, high, low))
    edge = exchange(spectra_half(True, voltages, taper, high, low, left, right, history))
    return correlate(inner, edge)


def solution(mesh):
    in_specs = (P("inp", "chan", None), P("inp", None, None), P())
    out_specs = P(None, ("inp", "chan"), None, None)
    return jax.shard_map(on_device, mesh=mesh, in_specs=in_specs, out_specs=out_specs, check_vma=False)
```

time: 608 us -> 142 us (0.23); the launches traced: 600 us -> 141 us
  matrix products: 238 us -> 0 us
  local copies, waits for them, and re-layouts: 194 us -> 11.4 us
  other arithmetic: 76.9 us -> 0 us
  Pallas kernels: 0 us -> 73.5 us
  waiting for transfers between devices: 62.2 us -> 0.01 us
  blocking collectives: 0 us -> 40.1 us
  starting transfers between devices: 23.1 us -> 16.3 us
  loops' own time: 6.22 us -> 0 us
    dot_general x16 -> x0, matrix products: 238 us -> none  [the longest x2 69.7 us: transform(): jnp.einsum('isan,ak->nksi', frames, first_cos, precision=highest)]
    pallas_call x0 -> x3, Pallas kernels: none -> 73.5 us  [the longest x2 58.4 us: spectra_half(): pl.pallas_call(functools.partial(spectra_kernel, edges), out_shape=jax.Sh...]
    add x2 -> x0, other arithmetic: 56 us -> none  [filter_step(): filtered + taper[offset][None, None, :] * slab[:, offset:offset + block_s...]
    unnamed x7 -> x2, local copies, waits for them, and re-layouts: 47.7 us -> 4.8 us
    ppermute x1 -> x2, waiting for transfers between devices: 40.1 us -> 0.01 us  [the longest x1 0.01 us: on_device(): left = lax.ppermute(left, 'chan', [(i, i + 1) for i in range(chan - 1)])]
    all_to_all x0 -> x1, blocking collectives: none -> 40.1 us  [exchange(): lax.all_to_all(value, ('inp', 'chan'), split_axis=0, concat_axis=0, tiled...]
    add x2 -> x0, local copies, waits for them, and re-layouts: 33.3 us -> none  [on_device(): vis_real = correlate(real_part, real_part) + correlate(imag_part, imag_part)]
    sub x2 -> x0, local copies, waits for them, and re-layouts: 33.1 us -> none  [on_device(): vis_imag = correlate(imag_part, real_part) - correlate(real_part, imag_part)]
  transfers between devices with their start and end apart: 3 -> 3, of which waited for: 3 -> 0; matrix products, arithmetic and copies ran while one was open for 6% -> 4% of each run, Pallas kernels for 0% -> 41%
where the time goes in v1:
time: 142 us; the launch traced here: 141 us
  Pallas kernels  73.5 us (52%)
  blocking collectives  40.1 us (28%)
  starting transfers between devices  16.3 us (11%)
  local copies, waits for them, and re-layouts  11.4 us (8%)
    pallas_call x2, Pallas kernels, spectra_half(): pl.pallas_call(functools.partial(spectra_kernel, edges), out_shape=jax.Sh...  58.4 us
    all_to_all x1, blocking collectives, exchange(): lax.all_to_all(value, ('inp', 'chan'), split_axis=0, concat_axis=0, tiled...  40.1 us
    pallas_call x1, Pallas kernels, correlate(): pl.pallas_call(correlate_kernel, grid=(16,), out_shape=jax.ShapeDtypeStru...  15.1 us
    all_to_all x1, starting transfers between devices, exchange(): lax.all_to_all(value, ('inp', 'chan'), split_axis=0, concat_axis=0, tiled...  11.8 us
    unnamed x2, local copies, waits for them, and re-layouts  4.8 us
    ppermute x1, starting transfers between devices, on_device(): left = lax.ppermute(left, 'chan', [(i, i + 1) for i in range(chan - 1)])  4.5 us
    slice x1, local copies, waits for them, and re-layouts, on_device(): left = jnp.transpose(voltages[:, SPECTRA - 4:], (1, 0, 2))  3.43 us
    slice x1, local copies, waits for them, and re-layouts, on_device(): right = jnp.transpose(voltages[:, :3], (1, 0, 2))  3.18 us
  transfers between devices with their start and end apart: 3, of which 0 were waited for; matrix products, arithmetic and copies ran while one was open for 4% of the time, Pallas kernels for 41%

profile of v1, /device:TPU:1, one launch (start us, length us, event | category | flops | bytes accessed | tf_op | source)
XLA Modules:
  0.0 141.4 jit_solution(10783510169723810040)
XLA Ops:
  0.0 3.4 %slice.6 = bf16[32,4,8192]{2,1,0:T(4,128)(2,1)S(1)} slice(bf16[32,16,8192]{2,1,0:T(8,128)(2,1)} %own_hbm.3), slice={[0:32], [12:16], [0:8192]} | slice | bytes 4194304 | tf_op jit(solution)/shard_map/slice | solution.py:286
  3.4 2.5 %copy.12 = bf16[32,4,8192]{2,0,1:T(8,128)(2,1)} copy(bf16[32,4,8192]{2,1,0:T(4,128)(2,1)S(1)} %slice.6) | data formatting | bytes 4194304
  5.9 4.5 %collective-permute-start = (bf16[4,32,8192]{2,1,0:T(8,128)(2,1)}, bf16[4,32,8192]{2,1,0:T(8,128)(2,1)}, u32[]{:S(2)}, u32[]{:S(2)}) collective-permute-start(bf16[4,32,8192]{2,1,0:T(8,128)(2,1)} %bitcast.5), channel_id=1, source_target_pairs={{0,1},{1,2},{2,3},{3,4},{4,5},{5,6},{6,7},{7,8},{8,9},{9,10},{10,1... | collective-permute-start | bytes 6291464 | tf_op jit(solution)/shard_map/ppermute | solution.py:288
  10.4 3.2 %slice.7 = bf16[32,3,8192]{2,1,0:T(4,128)(2,1)S(1)} slice(bf16[32,16,8192]{2,1,0:T(8,128)(2,1)} %own_hbm.3), slice={[0:32], [0:3], [0:8192]} | slice | bytes 3145728 | tf_op jit(solution)/shard_map/slice | solution.py:287
  13.6 2.3 %copy.13 = bf16[32,3,8192]{2,0,1:T(8,128)(2,1)} copy(bf16[32,3,8192]{2,1,0:T(4,128)(2,1)S(1)} %slice.7) | data formatting | bytes 3145728
  15.9 0.0 collective-permute-start.1
  15.9 27.0 %spectra_inner.1 = bf16[128,2,32,128]{3,2,1,0:T(8,128)(2,1)} custom-call(bf16[32,16,8192]{2,1,0:T(8,128)(2,1)} %own_hbm.3, f32[8,8192]{1,0:T(8,128)} %taper.3, bf16[16,256,512]{2,1,0:T(8,128)(2,1)} %constant.4.clone.high_hbm, bf16[16,256,512]{2,1,0:T(8,128)(2,1)} %constant.5.clone.low_hbm), custom_call_target="tpu_custom_call" | custom-call | flops 20000000000 | bytes 20000000 | tf_op jit(solution)/shard_map/spectra_inner/pallas_call | solution.py:211
  42.9 11.8 %all-to-all-start = ((bf16[128,2,32,128]{3,2,1,0:T(8,128)(2,1)}), bf16[128,2,32,128]{3,2,1,0:T(8,128)(2,1)S(1)}, u32[]{:S(2)}, u32[]{:S(2)}) async-start(bf16[128,2,32,128]{3,2,1,0:T(8,128)(2,1)} %spectra_inner.1), calls=%async_computation | async-start | bytes 4194304 | tf_op jit(solution)/shard_map/all_to_all | solution.py:293
  54.7 0.0 collective-permute-done.1.rest_1_
  54.8 0.0 collective-permute-done.rest_0_
  54.8 31.4 %spectra_edges.1 = bf16[128,2,32,128]{3,2,1,0:T(8,128)(2,1)} custom-call(bf16[32,16,8192]{2,1,0:T(8,128)(2,1)} %own_hbm.3, f32[8,8192]{1,0:T(8,128)} %taper.3, bf16[16,256,512]{2,1,0:T(8,128)(2,1)} %constant.4.clone.high_hbm, bf16[16,256,512]{2,1,0:T(8,128)(2,1)} %constant.5.clone.low_hbm, bf16[4,32,8192]{2,1,0:T(8,128)(2,1)} %collective-permute-done.rest_0_, ...), custom_call_target="tpu_custom_call" | custom-call | flops 20000000000 | bytes 20000000 | tf_op jit(solution)/shard_map/spectra_edges/pallas_call | solution.py:211
  86.2 0.0 all-to-all-done.first_ref
  86.2 40.1 %all_to_all.10.second_ref = bf16[128,2,32,128]{3,2,1,0:T(8,128)(2,1)S(1)} all-to-all(bf16[128,2,32,128]{3,2,1,0:T(8,128)(2,1)} %spectra_edges.1), channel_id=1, replica_groups=mesh['inp'=8,'chan'=16] {'inp','chan'}, dimensions={0} | all-to-all | bytes 4194304 | tf_op jit(solution)/shard_map/all_to_all | solution.py:293
  126.2 15.1 %correlate.1 = bf16[2,16,256,256]{3,2,1,0:T(8,128)(2,1)} custom-call(bf16[128,2,32,128]{3,2,1,0:T(8,128)(2,1)S(1)} %all-to-all-done.first_ref, bf16[128,2,32,128]{3,2,1,0:T(8,128)(2,1)S(1)} %all_to_all.10.second_ref), custom_call_target="tpu_custom_call" | custom-call | flops 4300000256 | bytes 9000000 | tf_op jit(solution)/shard_map/correlate/pallas_call | solution.py:270
Async XLA Ops:
  5.9 48.9 %collective-permute-start = (bf16[4,32,8192]{2,1,0:T(8,128)(2,1)}, bf16[4,32,8192]{2,1,0:T(8,128)(2,1)}, u32[]{:S(2)}, u32[]{:S(2)}) collective-permute-start(bf16[4,32,8192]{2,1,0:T(8,128)(2,1)} %bitcast.5), channel_id=1, source_target_pairs={{0,1},{1,2},{2,3},{3,4},{4,5},{5,6},{6,7},{7,8},{8,9},{9,10},{10,1... | collective-permute-start | bytes 6291464 | tf_op jit(solution)/shard_map/ppermute | solution.py:288
  15.9 38.8 %collective-permute-start.1 = (bf16[3,32,8192]{2,1,0:T(8,128)(2,1)}, bf16[3,32,8192]{2,1,0:T(8,128)(2,1)}, u32[]{:S(2)}, u32[]{:S(2)}) collective-permute-start(bf16[3,32,8192]{2,1,0:T(8,128)(2,1)} %bitcast.6), channel_id=1, source_target_pairs={{0,15},{1,0},{2,1},{3,2},{4,3},{5,4},{6,5},{7,6},{8,7},{9,8},{10,9... | collective-permute-start | bytes 4718600 | tf_op jit(solution)/shard_map/ppermute | solution.py:289
  42.9 43.2 %all-to-all-start = ((bf16[128,2,32,128]{3,2,1,0:T(8,128)(2,1)}), bf16[128,2,32,128]{3,2,1,0:T(8,128)(2,1)S(1)}, u32[]{:S(2)}, u32[]{:S(2)}) async-start(bf16[128,2,32,128]{3,2,1,0:T(8,128)(2,1)} %spectra_inner.1), calls=%async_computation | async-start | bytes 4194304 | tf_op jit(solution)/shard_map/all_to_all | solution.py:293

commit v2 on v1

v2 whole, which is shorter than its diff:
```python
import functools
import math

import jax
import jax.numpy as jnp
import ml_dtypes
import numpy as np
from jax import lax
from jax.experimental import pallas as pl
from jax.experimental.pallas import tpu as pltpu
from jax.sharding import PartitionSpec as P

FRAME = 8192
LOW = 1024
BAND = 2048
TAPS = 8
RADIX = 32
INNER = FRAME // RADIX
LANES = 128
NIN = 32
SPECTRA = 16
STRIDE = 17
GAP = 65

COLS = FRAME // LANES
SLOTS = 4
PIECES = 4


def second_stage_tables():
    m = np.arange(INNER, dtype=np.int64)
    k1 = LOW // RADIX + np.arange(BAND // RADIX, dtype=np.int64)

    def angles(k0):
        index = (m[None, :] * (k0 + RADIX * k1[:, None])) % FRAME
        angle = index * (2.0 * math.pi / FRAME)
        return np.cos(angle), np.sin(angle)

    table = np.zeros((RADIX // 2, 4, k1.size, 2, INNER))
    for k0 in range(1, RADIX // 2):
        cos, sin = angles(k0)
        table[k0, 0, :, 0], table[k0, 0, :, 1] = cos, sin
        table[k0, 1, :, 0], table[k0, 1, :, 1] = -sin, cos
        cos, sin = angles(RADIX - k0)
        table[k0, 2, :, 0], table[k0, 2, :, 1] = cos, -sin
        table[k0, 3, :, 0], table[k0, 3, :, 1] = -sin, -cos
    cos, sin = angles(0)
    table[0, 0, :, 0], table[0, 1, :, 0] = cos, -sin
    cos, sin = angles(RADIX // 2)
    table[0, 2, :, 1], table[0, 3, :, 1] = cos, -sin
    table = (table / math.sqrt(FRAME)).reshape(RADIX // 2, 4 * k1.size, 2 * INNER)
    table = table.astype(np.float32)
    high = table.astype(ml_dtypes.bfloat16)
    low = (table - high.astype(np.float32)).astype(ml_dtypes.bfloat16)
    return high, low


def real_fft(values):
    n = len(values)
    if n == 2:
        return [values[0] + values[1], values[0] - values[1]], [None, None]
    even_re, even_im = real_fft(values[0::2])
    odd_re, odd_im = real_fft(values[1::2])
    re, im = [None] * (n // 2 + 1), [None] * (n // 2 + 1)
    re[0], re[n // 2] = even_re[0] + odd_re[0], even_re[0] - odd_re[0]
    re[n // 4], im[n // 4] = even_re[n // 4], -odd_re[n // 4]
    for k in range(1, n // 4):
        cos, sin = math.cos(2 * math.pi * k / n), math.sin(2 * math.pi * k / n)
        if 8 * k == n:
            turned_re = (odd_re[k] + odd_im[k]) * cos
            turned_im = (odd_im[k] - odd_re[k]) * cos
        else:
            turned_re = odd_re[k] * cos + odd_im[k] * sin
            turned_im = odd_im[k] * cos - odd_re[k] * sin
        re[k], im[k] = even_re[k] + turned_re, even_im[k] + turned_im
        re[n // 2 - k], im[n // 2 - k] = even_re[k] - turned_re, turned_im - even_im[k]
    return re, im


def regroup(ref, rows, matrix, offset):
    lane = lax.broadcasted_iota(jnp.int32, (16, LANES), 1)
    lower = lane < 64
    even = lane % 64 < 32

    def step(index, carry):
        tile, part, quad = index // 4, (index // 2) % 2, index % 2
        for a in range(4):
            for src in range(16):
                value = ref[(quad * 4 + a) * 16 + src, tile, pl.ds(pl.multiple_of(part * 16, 16), 16), :]
                rows[pl.ds((a * 16 + src) * STRIDE, 16), :] = value.astype(jnp.float32)
        for c in range(16):
            t = [rows[pl.ds(a * 16 * STRIDE + c, 16, stride=STRIDE), :] for a in range(4)]
            u = [None] * 4
            for a in range(2):
                u[a] = jnp.where(lower, t[a], pltpu.roll(t[a + 2], 64, 1))
                u[a + 2] = jnp.where(lower, pltpu.roll(t[a], 64, 1), t[a + 2])
            for a in (0, 2):
                first = jnp.where(even, u[a], pltpu.roll(u[a + 1], 32, 1))
                second = jnp.where(even, pltpu.roll(u[a], 96, 1), u[a + 1])
                for b, value in enumerate((first, second)):
                    row = pl.ds(pl.multiple_of(offset + (tile * 4 + a + b) * 16, 16), 16)
                    lanes = pl.ds(pl.multiple_of(quad * LANES, LANES), LANES)
                    matrix[c, part, row, lanes] = value.astype(jnp.bfloat16)
        return carry

    lax.fori_loop(0, 8, step, 0)


def exchange(send, got, local_sem, send_sem, recv_sem):
    inp, chan = lax.axis_index("inp"), lax.axis_index("chan")
    me = inp * 16 + chan
    x, y, z, core = chan // 2 % 4, inp % 4, chan // 8 * 2 + inp // 4, chan % 2

    def step(n, carry):
        n = n * 37 % 128
        to_x, to_y, to_z = (x + n // 2 % 4) % 4, (y + n // 8 % 4) % 4, (z + n // 32) % 4
        to_inp, to_chan = to_z % 2 * 4 + to_y, to_z // 2 * 8 + to_x * 2 + (core + n) % 2
        pltpu.make_async_remote_copy(
            src_ref=send.at[to_inp * 16 + to_chan],
            dst_ref=got.at[me],
            send_sem=send_sem,
            recv_sem=recv_sem,
            device_id=(to_inp, to_chan),
            device_id_type=pl.DeviceIdType.MESH,
        ).start()
        return carry

    lax.fori_loop(1, 128, step, 0)
    local = pltpu.make_async_copy(send.at[me], got.at[me], local_sem)
    local.start()
    return local


def all_copies(send, got, send_sem, recv_sem):
    return pltpu.make_async_remote_copy(
        src_ref=send.at[pl.ds(0, 127)],
        dst_ref=got.at[pl.ds(0, 127)],
        send_sem=send_sem,
        recv_sem=recv_sem,
        device_id=(lax.axis_index("inp"), lax.axis_index("chan")),
        device_id_type=pl.DeviceIdType.MESH,
    )


def spectra_kernel(
    own_hbm, taper, high_hbm, low_hbm, history_hbm, matrix,
    own, history, left_send, right_send, left, right, high, low, rows, filtered, turned, gathered,
    sends, gots, load_sems, table_sems, halo_send_sems, halo_recv_sems, local_sems, send_sems, recv_sems,
):
    inp, chan = lax.axis_index("inp"), lax.axis_index("chan")
    chans = lax.axis_size("chan")
    first, last = chan == 0, chan == chans - 1
    width = FRAME // PIECES

    def loads(group, piece):
        inputs, lanes = pl.ds(16 * group, 16), pl.ds(width * piece, width)
        return pltpu.make_async_copy(own_hbm.at[inputs, :, lanes], own.at[inputs, :, lanes], load_sems.at[group, piece])

    tables = [
        pltpu.make_async_copy(high_hbm, high, table_sems.at[0]),
        pltpu.make_async_copy(low_hbm, low, table_sems.at[1]),
        pltpu.make_async_copy(history_hbm, history, table_sems.at[2]),
    ]
    for group in range(2):
        for piece in range(PIECES):
            loads(group, piece).start()
    for copy in tables:
        copy.start()

    def halo_copies(group, piece):
        at = (slice(None), pl.ds(16 * group, 16), pl.ds(width * piece, width))
        return [
            pltpu.make_async_remote_copy(
                src_ref=source.at[at],
                dst_ref=target.at[at],
                send_sem=halo_send_sems.at[n, group, piece],
                recv_sem=halo_recv_sems.at[n, group, piece],
                device_id=(inp, (chan + by) % chans),
                device_id_type=pl.DeviceIdType.MESH,
            )
            for n, (source, target, by) in enumerate(((left_send, left, 1), (right_send, right, chans - 1)))
        ]

    def column(group, col, slot):
        base = slot * 16 * STRIDE
        lanes = pl.ds(pl.multiple_of(col * LANES, LANES), LANES)
        for i in range(16):
            rows[pl.ds(base + i * STRIDE, 16), :] = own[group * 16 + i, :, lanes].astype(jnp.float32)

    def fir(edges, group, col, slot):
        base = slot * 16 * STRIDE
        lanes = pl.ds(pl.multiple_of(col * LANES, LANES), LANES)
        taps = taper[:, lanes]
        taps = [jnp.broadcast_to(taps[t : t + 1], (8, LANES)) for t in range(TAPS)]
        inputs = pl.ds(pl.multiple_of(group * 16, 16), 16)
        near = [rows[pl.ds(base + f, 16, stride=STRIDE), :] for f in range(16)]
        if edges:
            past = [history[f, inputs, lanes].astype(jnp.float32) for f in range(7)]
            before = [jnp.where(first, past[3 + f], left[f, inputs, lanes].astype(jnp.float32)) for f in range(4)]
            after = [right[f, inputs, lanes].astype(jnp.float32) for f in range(3)]
            start = before + near[:7]
            end = [jnp.where(last, past[f], near[9 + f]) for f in range(7)] + after
            windows = [start[o : o + TAPS] for o in range(4)] + [near[8:]] + [end[o : o + TAPS] for o in range(3)]
        else:
            for n in range(4):
                left_send[n, inputs, lanes] = near[12 + n].astype(jnp.bfloat16)
            for n in range(3):
                right_send[n, inputs, lanes] = near[n].astype(jnp.bfloat16)
            windows = [near[o : o + TAPS] for o in range(8)]
        for h in range(2):
            for o, window in enumerate(windows):
                total = window[0][8 * h : 8 * h + 8] * taps[0]
                for t in range(1, TAPS):
                    total = total + window[t][8 * h : 8 * h + 8] * taps[t]
                filtered[o, col, pl.ds(8 * h, 8), :] = total

    def half(edges, send):
        for group in range(2):
            def columns(step, carry):
                for slot in range(SLOTS):
                    column(group, step * SLOTS + slot, slot)
                for slot in range(SLOTS):
                    fir(edges, group, step * SLOTS + slot, slot)
                return carry

            for piece in range(PIECES):
                if edges:
                    for copy in halo_copies(group, piece):
                        copy.wait()
                else:
                    loads(group, piece).wait()
                steps = COLS // SLOTS // PIECES
                lax.fori_loop(piece * steps, (piece + 1) * steps, columns, 0)
                if not edges:
                    for copy in halo_copies(group, piece):
                        copy.start()

            def first_stage(o, carry):
                for part in range(2):
                    for h in range(2):
                        values = [filtered[o, 2 * a + part, pl.ds(8 * h, 8), :] for a in range(RADIX)]
                        re, im = real_fft(values)
                        im[0] = re[RADIX // 2]
                        row = pl.ds(pl.multiple_of(o * NIN + group * 16 + 8 * h, 8), 8)
                        for k in range(RADIX // 2):
                            turned[2 * k, row, part * LANES : (part + 1) * LANES] = re[k]
                            turned[2 * k + 1, row, part * LANES : (part + 1) * LANES] = im[k]
                return carry

            lax.fori_loop(0, 8, first_stage, 0)

        if not edges:
            for copy in tables:
                copy.wait()

        def second_stage(k, carry):
            both = jnp.concatenate([turned[2 * k], turned[2 * k + 1]], axis=1)
            both_high = both.astype(jnp.bfloat16)
            both_low = (both - both_high.astype(jnp.float32)).astype(jnp.bfloat16)

            def product(table, value):
                return lax.dot_general(table, value, (((1,), (1,)), ((), ())), preferred_element_type=jnp.float32)

            result = product(high[k], both_high) + product(high[k], both_low) + product(low[k], both_high)
            other = lax.rem(RADIX // 2 - k, RADIX // 2)
            for block in range(4):
                begin = 32 * (block // 2) + 16 * (block % 2) + (other if block >= 2 else k)
                for tile in range(2):
                    gathered[tile, pl.ds(begin, 64, stride=GAP), :] = result[
                        64 * block : 64 * block + 64, tile * LANES : (tile + 1) * LANES
                    ]
            return carry

        lax.fori_loop(0, RADIX // 2, second_stage, 0, unroll=4)

        def emit(block, carry):
            begin = pl.multiple_of(block * 8 * GAP, 8)
            for tile in range(2):
                for h in range(8):
                    value = gathered[tile, pl.ds(begin + h * GAP, 64), :].astype(jnp.bfloat16)
                    send[pl.ds(block * 16 + 2 * h, 2), tile] = value.reshape(2, 32, LANES)
            return carry

        lax.fori_loop(0, 8, emit, 0)

    locals_ = []
    for n in range(2):
        half(n == 1, sends.at[n])
        locals_.append(exchange(sends.at[n], gots.at[n], local_sems.at[n], send_sems.at[n], recv_sems.at[n]))
    for n in range(2):
        copies = all_copies(sends.at[n], gots.at[n], send_sems.at[n], recv_sems.at[n])
        copies.wait_recv()
        locals_[n].wait()
        regroup(gots.at[n], rows, matrix, 128 * n)
    for n in range(2):
        all_copies(sends.at[n], gots.at[n], send_sems.at[n], recv_sems.at[n]).wait_send()


def spectra(voltages, taper, high, low, history):
    any_space = pl.BlockSpec(memory_space=pl.ANY)
    vmem = pl.BlockSpec(memory_space=pltpu.VMEM)
    dma = pltpu.SemaphoreType.DMA
    return pl.pallas_call(
        spectra_kernel,
        out_shape=jax.ShapeDtypeStruct((16, 2, 256, 256), jnp.bfloat16),
        in_specs=[any_space, vmem, any_space, any_space, any_space],
        out_specs=vmem,
        scratch_shapes=[
            pltpu.VMEM((NIN, SPECTRA, FRAME), jnp.bfloat16),
            pltpu.VMEM((7, NIN, FRAME), jnp.bfloat16),
            pltpu.VMEM((4, NIN, FRAME), jnp.bfloat16),
            pltpu.VMEM((3, NIN, FRAME), jnp.bfloat16),
            pltpu.VMEM((4, NIN, FRAME), jnp.bfloat16),
            pltpu.VMEM((3, NIN, FRAME), jnp.bfloat16),
            pltpu.VMEM((16, 256, 512), jnp.bfloat16),
            pltpu.VMEM((16, 256, 512), jnp.bfloat16),
            pltpu.VMEM((SLOTS * 16 * STRIDE, LANES), jnp.float32),
            pltpu.VMEM((8, COLS, 16, LANES), jnp.float32),
            pltpu.VMEM((RADIX, 256, 256), jnp.float32),
            pltpu.VMEM((2, 64 * GAP, LANES), jnp.float32),
            pltpu.VMEM((2, 128, 2, 32, LANES), jnp.bfloat16),
            pltpu.VMEM((2, 128, 2, 32, LANES), jnp.bfloat16),
            dma((2, PIECES)),
            dma((3,)),
            dma((2, 2, PIECES)),
            dma((2, 2, PIECES)),
            dma((2,)),
            dma((2,)),
            dma((2,)),
        ],
        compiler_params=pltpu.CompilerParams(vmem_limit_bytes=60 << 20, has_side_effects=True),
        cost_estimate=pl.CostEstimate(flops=30_000_000_000, bytes_accessed=25_000_000, transcendentals=0),
        name="spectra",
    )(voltages, taper, high, low, history)


def correlate_kernel(matrix, out):
    def product(left, right):
        return lax.dot_general(left, right, (((1,), (0,)), ((), ())), preferred_element_type=jnp.float32)

    scale = 1.0 / 256.0
    for n in range(out.shape[1]):
        re, im = matrix[n, 0], matrix[n, 1]
        re_t, im_t = re.T, im.T
        out[0, n] = ((product(re_t, re) + product(im_t, im)) * scale).astype(jnp.bfloat16)
        out[1, n] = ((product(im_t, re) - product(re_t, im)) * scale).astype(jnp.bfloat16)


def correlate(matrix):
    return pl.pallas_call(
        correlate_kernel,
        grid=(4,),
        out_shape=jax.ShapeDtypeStruct((2, 16, 256, 256), jnp.bfloat16),
        in_specs=[pl.BlockSpec((4, 2, 256, 256), lambda c: (c, 0, 0, 0))],
        out_specs=pl.BlockSpec((2, 4, 256, 256), lambda c: (0, c, 0, 0)),
        compiler_params=pltpu.CompilerParams(vmem_limit_bytes=32 << 20),
        cost_estimate=pl.CostEstimate(flops=4_300_000_000, bytes_accessed=9_000_000, transcendentals=0),
        name="correlate",
    )(matrix)


def on_device(voltages, history, taper):
    high, low = (jnp.asarray(t) for t in second_stage_tables())
    return correlate(spectra(voltages, taper, high, low, jnp.transpose(history, (1, 0, 2))))


def solution(mesh):
    in_specs = (P("inp", "chan", None), P("inp", None, None), P())
    out_specs = P(None, ("inp", "chan"), None, None)
    return jax.shard_map(on_device, mesh=mesh, in_specs=in_specs, out_specs=out_specs, check_vma=False)
```

time: 142 us -> 102 us (0.72)
  blocking collectives: 40.1 us -> 0 us
  Pallas kernels: 73.5 us -> 99.9 us
  starting transfers between devices: 16.3 us -> 0 us
  local copies, waits for them, and re-layouts: 11.4 us -> 2.18 us
    all_to_all x1 -> x0, blocking collectives: 40.1 us -> none  [exchange(): lax.all_to_all(value, ('inp', 'chan'), split_axis=0, concat_axis=0, tiled...]
    pallas_call x3 -> x2, Pallas kernels: 73.5 us -> 99.9 us  [the longest x1 95.7 us: spectra(): pl.pallas_call(spectra_kernel, out_shape=jax.ShapeDtypeStruct((16, 2, 256...]
    all_to_all x1 -> x0, starting transfers between devices: 11.8 us -> none  [exchange(): lax.all_to_all(value, ('inp', 'chan'), split_axis=0, concat_axis=0, tiled...]
    slice x2 -> x0, local copies, waits for them, and re-layouts: 6.61 us -> none  [the longest x1 3.43 us: on_device(): left = jnp.transpose(voltages[:, SPECTRA - 4:], (1, 0, 2))]
    ppermute x2 -> x0, starting transfers between devices: 4.5 us -> none  [the longest x1 4.5 us: on_device(): left = lax.ppermute(left, 'chan', [(i, i + 1) for i in range(chan - 1)])]
    unnamed x2, local copies, waits for them, and re-layouts: 4.8 us -> 2.18 us
  transfers between devices with their start and end apart: 3 -> 0, of which waited for: 0 -> 0; matrix products, arithmetic and copies ran while one was open for 4% -> 0% of each run, Pallas kernels for 41% -> 0%
where the time goes in v2:
time: 102 us
  Pallas kernels  99.9 us (98%)
  local copies, waits for them, and re-layouts  2.18 us (2%)
    pallas_call x1, Pallas kernels, spectra(): pl.pallas_call(spectra_kernel, out_shape=jax.ShapeDtypeStruct((16, 2, 256...  95.7 us
    pallas_call x1, Pallas kernels, correlate(): pl.pallas_call(correlate_kernel, grid=(4,), out_shape=jax.ShapeDtypeStruc...  4.17 us
    unnamed x2, local copies, waits for them, and re-layouts  2.18 us

profile of v2, /device:TPU:1, one launch (start us, length us, event | category | flops | bytes accessed | tf_op | source)
XLA Modules:
  0.0 102.1 jit_solution(7053448770308673541)
XLA Ops:
  0.0 95.7 %spectra.1.matrix = bf16[16,2,256,256]{3,2,1,0:T(8,128)(2,1)} custom-call(bf16[32,16,8192]{2,1,0:T(8,128)(2,1)} %own_hbm.1, f32[8,8192]{1,0:T(8,128)} %taper.1, bf16[16,256,512]{2,1,0:T(8,128)(2,1)} %constant.4.clone.high_hbm, bf16[16,256,512]{2,1,0:T(8,128)(2,1)} %constant.5.clone.low_hbm, bf16[7,32,8192]{2,1,0:T(8,128)(2,1)} %bitcast.1), custom_call_target="tpu_custom_call" | custom-call | flops 30000001024 | bytes 25000000 | tf_op jit(solution)/shard_map/spectra/pallas_call | solution.py:303
  95.7 0.0 copy-start
  95.7 2.2 %copy-done = bf16[16,2,256,256]{3,2,1,0:T(8,128)(2,1)S(1)} copy-done((bf16[16,2,256,256]{3,2,1,0:T(8,128)(2,1)S(1)}, bf16[16,2,256,256]{3,2,1,0:T(8,128)(2,1)}, u32[]{:S(2)}) %copy-start) | copy-done | bytes 4194328
  97.9 4.2 %correlate.1 = bf16[2,16,256,256]{3,2,1,0:T(8,128)(2,1)} custom-call(bf16[16,2,256,256]{3,2,1,0:T(8,128)(2,1)S(1)} %copy-done), custom_call_target="tpu_custom_call" | custom-call | flops 4300000256 | bytes 9000000 | tf_op jit(solution)/shard_map/correlate/pallas_call | solution.py:350
Async XLA Ops:
  95.7 2.2 %copy-start = (bf16[16,2,256,256]{3,2,1,0:T(8,128)(2,1)S(1)}, bf16[16,2,256,256]{3,2,1,0:T(8,128)(2,1)}, u32[]{:S(2)}) copy-start(bf16[16,2,256,256]{3,2,1,0:T(8,128)(2,1)} %spectra.1.matrix) | copy-start | bytes 12582916

commit v3 on v2

--- a/solution.py
+++ b/solution.py
@@ -77,13 +77,14 @@
     return re, im
 
 
-def regroup(ref, rows, matrix, offset):
+def regroup(ref, rows, matrix, tile, offset, turn):
     lane = lax.broadcasted_iota(jnp.int32, (16, LANES), 1)
     lower = lane < 64
     even = lane % 64 < 32
+    ahead = lane % 32 >= 16
 
     def step(index, carry):
-        tile, part, quad = index // 4, (index // 2) % 2, index % 2
+        part, quad = index // 2, index % 2
         for a in range(4):
             for src in range(16):
                 value = ref[(quad * 4 + a) * 16 + src, tile, pl.ds(pl.multiple_of(part * 16, 16), 16), :]
@@ -97,27 +98,37 @@
             for a in (0, 2):
                 first = jnp.where(even, u[a], pltpu.roll(u[a + 1], 32, 1))
                 second = jnp.where(even, pltpu.roll(u[a], 96, 1), u[a + 1])
+                if turn and a == 0:
+                    first = jnp.where(ahead, pltpu.roll(first, 1, 0), first)
                 for b, value in enumerate((first, second)):
-                    row = pl.ds(pl.multiple_of(offset + (tile * 4 + a + b) * 16, 16), 16)
                     lanes = pl.ds(pl.multiple_of(quad * LANES, LANES), LANES)
-                    matrix[c, part, row, lanes] = value.astype(jnp.bfloat16)
+                    matrix[c, part, pl.ds(offset + (a + b) * 16, 16), lanes] = value.astype(jnp.bfloat16)
         return carry
 
-    lax.fori_loop(0, 8, step, 0)
-
-
-def exchange(send, got, local_sem, send_sem, recv_sem):
+    lax.fori_loop(0, 4, step, 0)
+
+
+def place():
     inp, chan = lax.axis_index("inp"), lax.axis_index("chan")
-    me = inp * 16 + chan
     x, y, z, core = chan // 2 % 4, inp % 4, chan // 8 * 2 + inp // 4, chan % 2
 
-    def step(n, carry):
+    def device(n):
         n = n * 37 % 128
         to_x, to_y, to_z = (x + n // 2 % 4) % 4, (y + n // 8 % 4) % 4, (z + n // 32) % 4
-        to_inp, to_chan = to_z % 2 * 4 + to_y, to_z // 2 * 8 + to_x * 2 + (core + n) % 2
+        return to_z % 2 * 4 + to_y, to_z // 2 * 8 + to_x * 2 + (core + n) % 2
+
+    return inp, chan, device
+
+
+def exchange(send, got, tiles, local_sem, send_sem, recv_sem):
+    inp, chan, device = place()
+    me = inp * 16 + chan
+
+    def step(n, carry):
+        to_inp, to_chan = device(n)
         pltpu.make_async_remote_copy(
-            src_ref=send.at[to_inp * 16 + to_chan],
-            dst_ref=got.at[me],
+            src_ref=send.at[to_inp * 16 + to_chan, tiles],
+            dst_ref=got.at[me, tiles],
             send_sem=send_sem,
             recv_sem=recv_sem,
             device_id=(to_inp, to_chan),
@@ -126,15 +137,15 @@
         return carry
 
     lax.fori_loop(1, 128, step, 0)
-    local = pltpu.make_async_copy(send.at[me], got.at[me], local_sem)
+    local = pltpu.make_async_copy(send.at[me, tiles], got.at[me, tiles], local_sem)
     local.start()
     return local
 
 
-def all_copies(send, got, send_sem, recv_sem):
+def all_copies(send, got, tiles, send_sem, recv_sem):
     return pltpu.make_async_remote_copy(
-        src_ref=send.at[pl.ds(0, 127)],
-        dst_ref=got.at[pl.ds(0, 127)],
+        src_ref=send.at[pl.ds(0, 127), tiles],
+        dst_ref=got.at[pl.ds(0, 127), tiles],
         send_sem=send_sem,
         recv_sem=recv_sem,
         device_id=(lax.axis_index("inp"), lax.axis_index("chan")),
@@ -143,11 +154,11 @@
 
 
 def spectra_kernel(
-    own_hbm, taper, high_hbm, low_hbm, history_hbm, matrix,
+    own_hbm, taper, high_hbm, low_hbm, history_hbm, matrix_hbm,
     own, history, left_send, right_send, left, right, high, low, rows, filtered, turned, gathered,
-    sends, gots, load_sems, table_sems, halo_send_sems, halo_recv_sems, local_sems, send_sems, recv_sems,
+    sends, gots, matrix, load_sems, table_sems, halo_send_sems, halo_recv_sems, local_sems, send_sems, recv_sems, out_sems,
 ):
-    inp, chan = lax.axis_index("inp"), lax.axis_index("chan")
+    inp, chan, device = place()
     chans = lax.axis_size("chan")
     first, last = chan == 0, chan == chans - 1
     width = FRAME // PIECES
@@ -167,18 +178,28 @@
     for copy in tables:
         copy.start()
 
+    barrier = pltpu.get_barrier_semaphore()
+
+    def greet(n, carry):
+        pl.semaphore_signal(barrier, inc=1, device_id=device(n), device_id_type=pl.DeviceIdType.MESH)
+        return carry
+
+    lax.fori_loop(1, 128, greet, 0)
+
     def halo_copies(group, piece):
-        at = (slice(None), pl.ds(16 * group, 16), pl.ds(width * piece, width))
+        inputs, lanes = pl.ds(16 * group, 16), pl.ds(width * piece, width)
         return [
             pltpu.make_async_remote_copy(
-                src_ref=source.at[at],
-                dst_ref=target.at[at],
+                src_ref=source.at[pl.ds(0, count), inputs, lanes],
+                dst_ref=target.at[pl.ds(0, count), inputs, lanes],
                 send_sem=halo_send_sems.at[n, group, piece],
                 recv_sem=halo_recv_sems.at[n, group, piece],
                 device_id=(inp, (chan + by) % chans),
                 device_id_type=pl.DeviceIdType.MESH,
             )
-            for n, (source, target, by) in enumerate(((left_send, left, 1), (right_send, right, chans - 1)))
+            for n, (source, target, by, count) in enumerate(
+                ((left_send, left, 1, 4 - group), (right_send, right, chans - 1, 3 + group))
+            )
         ]
 
     def column(group, col, slot):
@@ -194,17 +215,22 @@
         taps = [jnp.broadcast_to(taps[t : t + 1], (8, LANES)) for t in range(TAPS)]
         inputs = pl.ds(pl.multiple_of(group * 16, 16), 16)
         near = [rows[pl.ds(base + f, 16, stride=STRIDE), :] for f in range(16)]
+        earlier, later = 4 - group, 3 + group
         if edges:
             past = [history[f, inputs, lanes].astype(jnp.float32) for f in range(7)]
-            before = [jnp.where(first, past[3 + f], left[f, inputs, lanes].astype(jnp.float32)) for f in range(4)]
-            after = [right[f, inputs, lanes].astype(jnp.float32) for f in range(3)]
+            before = [left[f, inputs, lanes].astype(jnp.float32) for f in range(earlier)]
+            before = [jnp.where(first, past[7 - earlier + f], before[f]) for f in range(earlier)]
+            after = [right[f, inputs, lanes].astype(jnp.float32) for f in range(later)]
             start = before + near[:7]
             end = [jnp.where(last, past[f], near[9 + f]) for f in range(7)] + after
-            windows = [start[o : o + TAPS] for o in range(4)] + [near[8:]] + [end[o : o + TAPS] for o in range(3)]
+            windows = [start[o : o + TAPS] for o in range(earlier)] + [near[8:]]
+            windows += [end[o : o + TAPS] for o in range(3)]
+            if group == 1:
+                windows = [end[3:]] + windows
         else:
-            for n in range(4):
-                left_send[n, inputs, lanes] = near[12 + n].astype(jnp.bfloat16)
-            for n in range(3):
+            for n in range(earlier):
+                left_send[n, inputs, lanes] = near[SPECTRA - earlier + n].astype(jnp.bfloat16)
+            for n in range(later):
                 right_send[n, inputs, lanes] = near[n].astype(jnp.bfloat16)
             windows = [near[o : o + TAPS] for o in range(8)]
         for h in range(2):
@@ -214,7 +240,7 @@
                     total = total + window[t][8 * h : 8 * h + 8] * taps[t]
                 filtered[o, col, pl.ds(8 * h, 8), :] = total
 
-    def half(edges, send):
+    def half(edges):
         for group in range(2):
             def columns(step, carry):
                 for slot in range(SLOTS):
@@ -232,6 +258,8 @@
                 steps = COLS // SLOTS // PIECES
                 lax.fori_loop(piece * steps, (piece + 1) * steps, columns, 0)
                 if not edges:
+                    if group == 0 and piece == 0:
+                        pl.semaphore_wait(barrier, 127)
                     for copy in halo_copies(group, piece):
                         copy.start()
 
@@ -273,27 +301,40 @@
 
         lax.fori_loop(0, RADIX // 2, second_stage, 0, unroll=4)
 
-        def emit(block, carry):
+    def emit(send, tile):
+        def step(block, carry):
             begin = pl.multiple_of(block * 8 * GAP, 8)
-            for tile in range(2):
-                for h in range(8):
-                    value = gathered[tile, pl.ds(begin + h * GAP, 64), :].astype(jnp.bfloat16)
-                    send[pl.ds(block * 16 + 2 * h, 2), tile] = value.reshape(2, 32, LANES)
+            for h in range(8):
+                value = gathered[tile, pl.ds(begin + h * GAP, 64), :].astype(jnp.bfloat16)
+                send[pl.ds(block * 16 + 2 * h, 2), tile] = value.reshape(2, 32, LANES)
             return carry
 
-        lax.fori_loop(0, 8, emit, 0)
-
-    locals_ = []
-    for n in range(2):
-        half(n == 1, sends.at[n])
-        locals_.append(exchange(sends.at[n], gots.at[n], local_sems.at[n], send_sems.at[n], recv_sems.at[n]))
-    for n in range(2):
-        copies = all_copies(sends.at[n], gots.at[n], send_sems.at[n], recv_sems.at[n])
-        copies.wait_recv()
-        locals_[n].wait()
-        regroup(gots.at[n], rows, matrix, 128 * n)
-    for n in range(2):
-        all_copies(sends.at[n], gots.at[n], send_sems.at[n], recv_sems.at[n]).wait_send()
+        lax.fori_loop(0, 8, step, 0)
+
+    chunks = [(0, pl.ds(0, 2)), (1, pl.ds(0, 1)), (1, pl.ds(1, 1))]
+    local_copies = []
+    half(False)
+    for n, (which, tiles) in enumerate(chunks):
+        if n == 1:
+            half(True)
+        for tile in range(tiles.start, tiles.start + tiles.size):
+            emit(sends.at[which], tile)
+        local_copies.append(
+            exchange(sends.at[which], gots.at[which], tiles, local_sems.at[n], send_sems.at[n], recv_sems.at[n])
+        )
+    writes = []
+    for n, (which, tiles) in enumerate(chunks):
+        all_copies(sends.at[which], gots.at[which], tiles, send_sems.at[n], recv_sems.at[n]).wait_recv()
+        local_copies[n].wait()
+        begin = 128 * which + 64 * tiles.start
+        for tile in range(tiles.start, tiles.start + tiles.size):
+            regroup(gots.at[which], rows, matrix, tile, 128 * which + 64 * tile, (which, tile) == (1, 0))
+        block = (slice(None), slice(None), pl.ds(begin, 64 * tiles.size))
+        writes.append(pltpu.make_async_copy(matrix.at[block], matrix_hbm.at[block], out_sems.at[n]))
+        writes[-1].start()
+    for n, (which, tiles) in enumerate(chunks):
+        all_copies(sends.at[which], gots.at[which], tiles, send_sems.at[n], recv_sems.at[n]).wait_send()
+        writes[n].wait()
 
 
 def spectra(voltages, taper, high, low, history):
@@ -304,14 +345,11 @@
         spectra_kernel,
         out_shape=jax.ShapeDtypeStruct((16, 2, 256, 256), jnp.bfloat16),
         in_specs=[any_space, vmem, any_space, any_space, any_space],
-        out_specs=vmem,
+        out_specs=any_space,
         scratch_shapes=[
             pltpu.VMEM((NIN, SPECTRA, FRAME), jnp.bfloat16),
             pltpu.VMEM((7, NIN, FRAME), jnp.bfloat16),
-            pltpu.VMEM((4, NIN, FRAME), jnp.bfloat16),
-            pltpu.VMEM((3, NIN, FRAME), jnp.bfloat16),
-            pltpu.VMEM((4, NIN, FRAME), jnp.bfloat16),
-            pltpu.VMEM((3, NIN, FRAME), jnp.bfloat16),
+            *[pltpu.VMEM((4, NIN, FRAME), jnp.bfloat16) for _ in range(4)],
             pltpu.VMEM((16, 256, 512), jnp.bfloat16),
             pltpu.VMEM((16, 256, 512), jnp.bfloat16),
             pltpu.VMEM((SLOTS * 16 * STRIDE, LANES), jnp.float32),
@@ -320,15 +358,17 @@
             pltpu.VMEM((2, 64 * GAP, LANES), jnp.float32),
             pltpu.VMEM((2, 128, 2, 32, LANES), jnp.bfloat16),
             pltpu.VMEM((2, 128, 2, 32, LANES), jnp.bfloat16),
+            pltpu.VMEM((16, 2, 256, 256), jnp.bfloat16),
             dma((2, PIECES)),
             dma((3,)),
             dma((2, 2, PIECES)),
             dma((2, 2, PIECES)),
-            dma((2,)),
-            dma((2,)),
-            dma((2,)),
+            dma((3,)),
+            dma((3,)),
+            dma((3,)),
+            dma((3,)),
         ],
-        compiler_params=pltpu.CompilerParams(vmem_limit_bytes=60 << 20, has_side_effects=True),
+        compiler_params=pltpu.CompilerParams(vmem_limit_bytes=60 << 20, has_side_effects=True, collective_id=0),
         cost_estimate=pl.CostEstimate(flops=30_000_000_000, bytes_accessed=25_000_000, transcendentals=0),
         name="spectra",
     )(voltages, taper, high, low, history)
@@ -349,11 +389,11 @@
 def correlate(matrix):
     return pl.pallas_call(
         correlate_kernel,
-        grid=(4,),
+        grid=(2,),
         out_shape=jax.ShapeDtypeStruct((2, 16, 256, 256), jnp.bfloat16),
-        in_specs=[pl.BlockSpec((4, 2, 256, 256), lambda c: (c, 0, 0, 0))],
-        out_specs=pl.BlockSpec((2, 4, 256, 256), lambda c: (0, c, 0, 0)),
-        compiler_params=pltpu.CompilerParams(vmem_limit_bytes=32 << 20),
+        in_specs=[pl.BlockSpec((8, 2, 256, 256), lambda c: (c, 0, 0, 0))],
+        out_specs=pl.BlockSpec((2, 8, 256, 256), lambda c: (0, c, 0, 0)),
+        compiler_params=pltpu.CompilerParams(vmem_limit_bytes=60 << 20),
         cost_estimate=pl.CostEstimate(flops=4_300_000_000, bytes_accessed=9_000_000, transcendentals=0),
         name="correlate",
     )(matrix)

time: 102 us -> 96.5 us (0.946)
  the two profiles are of different devices: /device:TPU:1 before, /device:TPU:7 now
where the time goes in v3:
time: 96.5 us; the launch traced here: 96.4 us
  Pallas kernels  96.3 us (100%)
    pallas_call x1, Pallas kernels, spectra(): pl.pallas_call(spectra_kernel, out_shape=jax.ShapeDtypeStruct((16, 2, 256...  90.8 us
    pallas_call x1, Pallas kernels, correlate(): pl.pallas_call(correlate_kernel, grid=(2,), out_shape=jax.ShapeDtypeStruc...  5.51 us

profile of v3, /device:TPU:7, one launch (start us, length us, event | category | flops | bytes accessed | tf_op | source)
XLA Modules:
  0.0 96.4 jit_solution(6718968866724849305)
XLA Ops:
  0.0 90.8 %spectra.1.matrix = bf16[16,2,256,256]{3,2,1,0:T(8,128)(2,1)} custom-call(bf16[32,16,8192]{2,1,0:T(8,128)(2,1)} %own_hbm.1, f32[8,8192]{1,0:T(8,128)} %taper.1, bf16[16,256,512]{2,1,0:T(8,128)(2,1)} %constant.4.clone.high_hbm, bf16[16,256,512]{2,1,0:T(8,128)(2,1)} %constant.5.clone.low_hbm, bf16[7,32,8192]{2,1,0:T(8,128)(2,1)} %bitcast.1), custom_call_target="tpu_custom_call" | custom-call | flops 30000001024 | bytes 25000000 | tf_op jit(solution)/shard_map/spectra/pallas_call | solution.py:344
  90.8 5.5 %correlate.1 = bf16[2,16,256,256]{3,2,1,0:T(8,128)(2,1)} custom-call(bf16[16,2,256,256]{3,2,1,0:T(8,128)(2,1)} %spectra.1.matrix), custom_call_target="tpu_custom_call" | custom-call | flops 4300000256 | bytes 9000000 | tf_op jit(solution)/shard_map/correlate/pallas_call | solution.py:390

commit v4 on v3

--- a/solution.py
+++ b/solution.py
@@ -110,12 +110,13 @@
 
 def place():
     inp, chan = lax.axis_index("inp"), lax.axis_index("chan")
+    rem, div = lax.rem, lax.div
     x, y, z, core = chan // 2 % 4, inp % 4, chan // 8 * 2 + inp // 4, chan % 2
 
     def device(n):
-        n = n * 37 % 128
-        to_x, to_y, to_z = (x + n // 2 % 4) % 4, (y + n // 8 % 4) % 4, (z + n // 32) % 4
-        return to_z % 2 * 4 + to_y, to_z // 2 * 8 + to_x * 2 + (core + n) % 2
+        n = rem(n * 27, 128)
+        to_x, to_y, to_z = rem(x + div(n, 2), 4), rem(y + div(n, 8), 4), rem(z + div(n, 32), 4)
+        return rem(to_z, 2) * 4 + to_y, div(to_z, 2) * 8 + to_x * 2 + rem(core + n, 2)
 
     return inp, chan, device
 
@@ -158,7 +159,7 @@
     own, history, left_send, right_send, left, right, high, low, rows, filtered, turned, gathered,
     sends, gots, matrix, load_sems, table_sems, halo_send_sems, halo_recv_sems, local_sems, send_sems, recv_sems, out_sems,
 ):
-    inp, chan, device = place()
+    inp, chan, _ = place()
     chans = lax.axis_size("chan")
     first, last = chan == 0, chan == chans - 1
     width = FRAME // PIECES
@@ -180,11 +181,11 @@
 
     barrier = pltpu.get_barrier_semaphore()
 
-    def greet(n, carry):
-        pl.semaphore_signal(barrier, inc=1, device_id=device(n), device_id_type=pl.DeviceIdType.MESH)
-        return carry
-
-    lax.fori_loop(1, 128, greet, 0)
+    inps = [lax.rem(inp + n, lax.axis_size("inp")) for n in range(lax.axis_size("inp"))]
+    chan_list = [lax.rem(chan + n, chans) for n in range(chans)]
+    for n in range(1, 128):
+        there = (inps[n // chans], chan_list[n % chans])
+        pl.semaphore_signal(barrier, inc=1, device_id=there, device_id_type=pl.DeviceIdType.MESH)
 
     def halo_copies(group, piece):
         inputs, lanes = pl.ds(16 * group, 16), pl.ds(width * piece, width)

time: 96.5 us -> 89.1 us (0.923)
  the two profiles are of different devices: /device:TPU:7 before, /device:TPU:1 now
where the time goes in v4:
time: 89.1 us; the launch traced here: 88.6 us
  Pallas kernels  88.6 us (99%)
    pallas_call x1, Pallas kernels, spectra(): pl.pallas_call(spectra_kernel, out_shape=jax.ShapeDtypeStruct((16, 2, 256...  83.1 us
    pallas_call x1, Pallas kernels, correlate(): pl.pallas_call(correlate_kernel, grid=(2,), out_shape=jax.ShapeDtypeStruc...  5.51 us

profile of v4, /device:TPU:1, one launch (start us, length us, event | category | flops | bytes accessed | tf_op | source)
XLA Modules:
  0.0 88.6 jit_solution(1055429672964538360)
XLA Ops:
  0.0 83.1 %spectra.1.matrix = bf16[16,2,256,256]{3,2,1,0:T(8,128)(2,1)} custom-call(bf16[32,16,8192]{2,1,0:T(8,128)(2,1)} %own_hbm.1, f32[8,8192]{1,0:T(8,128)} %taper.1, bf16[16,256,512]{2,1,0:T(8,128)(2,1)} %constant.4.clone.high_hbm, bf16[16,256,512]{2,1,0:T(8,128)(2,1)} %constant.5.clone.low_hbm, bf16[7,32,8192]{2,1,0:T(8,128)(2,1)} %bitcast.1), custom_call_target="tpu_custom_call" | custom-call | flops 30000001024 | bytes 25000000 | tf_op jit(solution)/shard_map/spectra/pallas_call | solution.py:345
  83.1 5.5 %correlate.1 = bf16[2,16,256,256]{3,2,1,0:T(8,128)(2,1)} custom-call(bf16[16,2,256,256]{3,2,1,0:T(8,128)(2,1)} %spectra.1.matrix), custom_call_target="tpu_custom_call" | custom-call | flops 4300000256 | bytes 9000000 | tf_op jit(solution)/shard_map/correlate/pallas_call | solution.py:391

commit v5 on v4

--- a/solution.py
+++ b/solution.py
@@ -111,12 +111,14 @@
 def place():
     inp, chan = lax.axis_index("inp"), lax.axis_index("chan")
     rem, div = lax.rem, lax.div
-    x, y, z, core = chan // 2 % 4, inp % 4, chan // 8 * 2 + inp // 4, chan % 2
+    x, y, z, core = rem(div(chan, 2), 4), rem(inp, 4), div(chan, 8) * 2 + div(inp, 4), rem(chan, 2)
+    xs, ys, zs = ([rem(v + n, 4) for n in range(4)] for v in (x, y, z))
+    highs, lows = [div(v, 2) * 8 for v in zs], [rem(v, 2) * 4 for v in zs]
+    pairs = [[v * 2 + rem(core + n, 2) for n in range(2)] for v in xs]
 
     def device(n):
-        n = rem(n * 27, 128)
-        to_x, to_y, to_z = rem(x + div(n, 2), 4), rem(y + div(n, 8), 4), rem(z + div(n, 32), 4)
-        return rem(to_z, 2) * 4 + to_y, div(to_z, 2) * 8 + to_x * 2 + rem(core + n, 2)
+        n = n * 27 % 128
+        return lows[n // 32] + ys[n // 8 % 4], highs[n // 32] + pairs[n // 2 % 4][n % 2]
 
     return inp, chan, device
 
@@ -125,7 +127,7 @@
     inp, chan, device = place()
     me = inp * 16 + chan
 
-    def step(n, carry):
+    for n in range(1, 128):
         to_inp, to_chan = device(n)
         pltpu.make_async_remote_copy(
             src_ref=send.at[to_inp * 16 + to_chan, tiles],
@@ -135,9 +137,6 @@
             device_id=(to_inp, to_chan),
             device_id_type=pl.DeviceIdType.MESH,
         ).start()
-        return carry
-
-    lax.fori_loop(1, 128, step, 0)
     local = pltpu.make_async_copy(send.at[me, tiles], got.at[me, tiles], local_sem)
     local.start()
     return local
@@ -173,11 +172,8 @@
         pltpu.make_async_copy(low_hbm, low, table_sems.at[1]),
         pltpu.make_async_copy(history_hbm, history, table_sems.at[2]),
     ]
-    for group in range(2):
-        for piece in range(PIECES):
-            loads(group, piece).start()
-    for copy in tables:
-        copy.start()
+    for piece in range(PIECES):
+        loads(0, piece).start()
 
     barrier = pltpu.get_barrier_semaphore()
 
@@ -256,6 +252,11 @@
                         copy.wait()
                 else:
                     loads(group, piece).wait()
+                    if group == 0:
+                        loads(1, piece).start()
+                    elif piece == 0:
+                        for copy in tables:
+                            copy.start()
                 steps = COLS // SLOTS // PIECES
                 lax.fori_loop(piece * steps, (piece + 1) * steps, columns, 0)
                 if not edges:

time: 89.1 us -> 88.6 us (level)
  no operation moved by 1% of the time
where the time goes in v5:
time: 88.6 us; the launch traced here: 88.5 us
  Pallas kernels  88.5 us (100%)
    pallas_call x1, Pallas kernels, spectra(): pl.pallas_call(spectra_kernel, out_shape=jax.ShapeDtypeStruct((16, 2, 256...  83 us
    pallas_call x1, Pallas kernels, correlate(): pl.pallas_call(correlate_kernel, grid=(2,), out_shape=jax.ShapeDtypeStruc...  5.51 us

profile of v5, /device:TPU:1, one launch (start us, length us, event | category | flops | bytes accessed | tf_op | source)
XLA Modules:
  0.0 88.5 jit_solution(17289975136050012778)
XLA Ops:
  0.0 83.0 %spectra.1.matrix = bf16[16,2,256,256]{3,2,1,0:T(8,128)(2,1)} custom-call(bf16[32,16,8192]{2,1,0:T(8,128)(2,1)} %own_hbm.1, f32[8,8192]{1,0:T(8,128)} %taper.1, bf16[16,256,512]{2,1,0:T(8,128)(2,1)} %constant.4.clone.high_hbm, bf16[16,256,512]{2,1,0:T(8,128)(2,1)} %constant.5.clone.low_hbm, bf16[7,32,8192]{2,1,0:T(8,128)(2,1)} %bitcast.1), custom_call_target="tpu_custom_call" | custom-call | flops 30000001024 | bytes 25000000 | tf_op jit(solution)/shard_map/spectra/pallas_call | solution.py:346
  83.0 5.5 %correlate.1 = bf16[2,16,256,256]{3,2,1,0:T(8,128)(2,1)} custom-call(bf16[16,2,256,256]{3,2,1,0:T(8,128)(2,1)} %spectra.1.matrix), custom_call_target="tpu_custom_call" | custom-call | flops 4300000256 | bytes 9000000 | tf_op jit(solution)/shard_map/correlate/pallas_call | solution.py:392
